TPU v7x, 32 devices: a whole 2x2x4 slice. The times are simulated.
32 devices in a mesh: seq: 16 (over z, y, core), head: 2 (over x).
Axes of the slice: x: 2, y: 2, z: 4, core: 2. Of those that a mesh axis runs over, the one named last changes fastest.
Arguments:
- tokens: bfloat16 [8192, 2048], P('seq', 'head'), may hold values from -200 to 200
- norm_gain: float32 [2, 2048], replicated, may hold values from 0.25 to 1.75
- w_query: bfloat16 [2, 2048, 2048], P(None, None, 'head'), may hold values from -0.35 to 0.35
- key_projection_weight: bfloat16 [2, 2048, 512], P(None, None, 'head'), may hold values from -0.35 to 0.35
- value_projection_weight: bfloat16 [2, 2048, 512], P(None, None, 'head'), may hold values from -0.125 to 0.125
- w_out: bfloat16 [2, 2048, 2048], P(None, 'head'), may hold values from -0.125 to 0.125
- counts: int32 [16], replicated, may hold values from 128 to 512
Outputs:
- hidden_out: bfloat16 [8192, 2048], P('seq', 'head')
Inputs may be any that keep to these rules, and one draw needn't show every extreme that they name: The first counts[b] tokens of block b of 512 positions are valid keys; the rest of the block is padding that no query uses as a key.
All inputs are finite; a program needn't handle non-finite values.
Results may differ from a plain program's by a relative error of at most 0.02.
The roundings to bfloat16 on the way count: a program that leaves them out, or rounds other values in their place, can miss the bound.
Values may be sent and summed in bfloat16 or wider, within the bound.
A program may use at most 128 MiB of HBM per device.

v0:
```python
import math
import jax
import jax.numpy as jnp
from jax import lax
from jax.sharding import PartitionSpec as P

MODEL_WIDTH = 2048
HEAD_SIZE = 128
WINDOW = 4096
LAYER_COUNT = 2
norm_epsilon = 1e-05
rope_base = 10000.0


def passed_along(value, axis, steps):
    count = lax.axis_size(axis)
    initial, last = (max(0, -steps), min(count, count - steps))
    return lax.ppermute(value, axis, [(source, source + steps) for source in range(initial, last)])


def rotate_heads(projected, token_positions, head_count):
    row_total = projected.shape[0]
    shaped = projected.reshape(row_total, head_count, HEAD_SIZE)
    half_dim = HEAD_SIZE // 2
    inverse = jnp.power(
        jnp.float32(rope_base), -2.0 * jnp.arange(half_dim, dtype=jnp.float32) / HEAD_SIZE
    )
    angles = token_positions.astype(jnp.float32)[:, None] * inverse[None, :]
    cosine_table = jnp.cos(angles)[:, None, :]
    sine_table = jnp.sin(angles)[:, None, :]
    first_half = shaped[..., :half_dim]
    second_half = shaped[..., half_dim:]
    rotated = jnp.concatenate(
        [
            first_half * cosine_table - second_half * sine_table,
            second_half * cosine_table + first_half * sine_table,
        ],
        axis=-1,
    )
    return rotated.astype(jnp.bfloat16)


def block_mask(counts, block_index, rows_here, span_blocks):
    key_length = (span_blocks + 1) * rows_here
    first_row = block_index * rows_here
    query_positions = first_row + jnp.arange(rows_here, dtype=jnp.int32)
    key_positions = first_row - span_blocks * rows_here + jnp.arange(key_length, dtype=jnp.int32)
    block_numbers = block_index - span_blocks + jnp.arange(span_blocks + 1, dtype=jnp.int32)
    table_size = counts.shape[0]
    matches = block_numbers[:, None] == jnp.arange(table_size, dtype=jnp.int32)[None, :]
    block_counts = jnp.sum(jnp.where(matches, counts[None, :], 0), axis=1)
    within_block = jnp.arange(rows_here, dtype=jnp.int32)
    valid_keys = (
        (block_numbers[:, None] >= 0) & (within_block[None, :] < block_counts[:, None])
    ).reshape(key_length)
    allowed = valid_keys[None, :] & (key_positions[None, :] <= query_positions[:, None])
    return allowed & (query_positions[:, None] - key_positions[None, :] < WINDOW)


def attend_local(queries, stacked, allowed):
    rows_here = queries.shape[0]
    local_heads = queries.shape[1]
    block_total = stacked.shape[0]
    local_groups = stacked.shape[3] // HEAD_SIZE
    key_length = block_total * rows_here
    key_heads = stacked[:, 0].reshape(key_length, local_groups, HEAD_SIZE).transpose(1, 0, 2)
    value_heads = stacked[:, 1].reshape(key_length, local_groups, HEAD_SIZE).transpose(1, 0, 2)
    query_heads = queries.transpose(1, 0, 2)
    group_length = local_heads // local_groups
    scale_factor = 1.0 / math.sqrt(HEAD_SIZE)

    def one_head(head_number):
        query_one = lax.dynamic_index_in_dim(query_heads, head_number, 0, keepdims=False)
        key_one = lax.dynamic_index_in_dim(
            key_heads, head_number // group_length, 0, keepdims=False
        )
        value_one = lax.dynamic_index_in_dim(
            value_heads, head_number // group_length, 0, keepdims=False
        )
        scores = (
            lax.dot_general(
                query_one, key_one, (((1,), (1,)), ((), ())), preferred_element_type=jnp.float32
            )
            * scale_factor
        )
        scores = jnp.where(allowed, scores, -jnp.inf)
        largest = jnp.max(scores, axis=1, keepdims=True)
        weights = jnp.exp(scores - largest)
        weights = (weights / jnp.sum(weights, axis=1, keepdims=True)).astype(jnp.bfloat16)
        return jnp.dot(weights, value_one, preferred_element_type=jnp.float32).astype(jnp.bfloat16)

    blended = lax.map(one_head, jnp.arange(local_heads, dtype=jnp.int32))
    return blended.transpose(1, 0, 2).reshape(rows_here, local_heads * HEAD_SIZE)


def relay_blocks(stacked_own, span_blocks):
    zero_blocks = jnp.zeros((span_blocks,) + stacked_own.shape, stacked_own.dtype)

    def step_once(step_number, carried):
        passing, collected = carried
        passing = passed_along(passing, "seq", 1)
        collected = lax.dynamic_update_index_in_dim(
            collected, passing, span_blocks - 1 - step_number, 0
        )
        return (passing, collected)

    passing, collected = lax.fori_loop(0, span_blocks, step_once, (stacked_own, zero_blocks))
    return jnp.concatenate([collected, stacked_own[None]], axis=0)


def per_device(
    tokens, norm_gain, w_query, key_projection_weight, value_projection_weight, w_out, counts
):
    rows_here = tokens.shape[0]
    half_width = tokens.shape[1]
    span_blocks = WINDOW // rows_here
    block_index = lax.axis_index("seq")
    head_index = lax.axis_index("head")
    token_positions = block_index * rows_here + jnp.arange(rows_here, dtype=jnp.int32)
    allowed = block_mask(counts, block_index, rows_here, span_blocks)
    local_query = w_query.shape[2] // HEAD_SIZE
    local_kv = key_projection_weight.shape[2] // HEAD_SIZE
    hidden = tokens
    for layer_position in range(LAYER_COUNT):
        gain_row = norm_gain[layer_position]
        query_weight = w_query[layer_position]
        key_weight = key_projection_weight[layer_position]
        value_weight = value_projection_weight[layer_position]
        widened = hidden.astype(jnp.float32)
        total_squares = lax.psum(jnp.sum(widened * widened, axis=1), "head")
        gain_part = lax.dynamic_slice_in_dim(gain_row, head_index * half_width, half_width, 0)
        normed_part = (
            widened
            * lax.rsqrt(total_squares / MODEL_WIDTH + norm_epsilon)[:, None]
            * gain_part[None, :]
        ).astype(jnp.bfloat16)

        def project_piece(
            running, piece_rows, offset, weights_now=(query_weight, key_weight, value_weight)
        ):
            width_here = piece_rows.shape[1]
            return tuple(
                (
                    jnp.dot(piece_rows, weight, preferred_element_type=jnp.float32)
                    for weight in weights_now
                )
            )

        starting = (
            jnp.zeros((rows_here, query_weight.shape[1]), jnp.float32),
            jnp.zeros((rows_here, key_weight.shape[1]), jnp.float32),
            jnp.zeros((rows_here, value_weight.shape[1]), jnp.float32),
        )
        query_raw, key_raw, value_raw = project_piece(
            starting, lax.all_gather(normed_part, "head", axis=1, tiled=True), jnp.int32(0)
        )
        queries = rotate_heads(query_raw, token_positions, local_query)
        keys_own = rotate_heads(key_raw, token_positions, local_kv).reshape(
            rows_here, local_kv * HEAD_SIZE
        )
        values_own = value_raw.astype(jnp.bfloat16)
        stacked_own = jnp.stack([keys_own, values_own])
        stacked = relay_blocks(stacked_own, span_blocks)
        attended = attend_local(queries, stacked, allowed)
        partial_product = jnp.dot(
            attended, w_out[layer_position], preferred_element_type=jnp.float32
        )
        rounded = lax.optimization_barrier(partial_product.astype(jnp.bfloat16)).astype(jnp.float32)
        own_share = lax.psum_scatter(
            rounded.astype(jnp.bfloat16), "head", scatter_dimension=1, tiled=True
        ).astype(jnp.float32)
        hidden = (hidden.astype(jnp.float32) + own_share).astype(jnp.bfloat16)
    return hidden


def solution(mesh):
    return jax.shard_map(
        per_device,
        mesh=mesh,
        in_specs=(
            P("seq", "head"),
            P(),
            P(None, None, "head"),
            P(None, None, "head"),
            P(None, None, "head"),
            P(None, "head", None),
            P(),
        ),
        out_specs=P("seq", "head"),
        check_vma=False,
    )
```

profile of v0, /device:TPU:0, one launch (start us, length us, event | category | flops | bytes accessed | tf_op | source)
XLA Modules:
  0.0 653.0 jit_solution(17317574865191985672)
XLA Ops:
  25.7 6.7 %copy.30 = bf16[1024,2048]{1,0:T(8,128)(2,1)} copy(bf16[1024,2048]{0,1:T(8,128)(2,1)} %get-tuple-element.469) | data formatting | bytes 8388608 | tf_op jit(solution)/shard_map/dot_general | solution.py:144
  34.5 17.8 %all-gather.3.cloned.1.call-done = bf16[512,2048]{1,0:T(8,128)(2,1)} async-done(((bf16[512,1024]{1,0:T(8,128)(2,1)}), bf16[512,2048]{1,0:T(8,128)(2,1)}) %all-gather.3.cloned.1.call-update) | async-done | bytes 2097168 | tf_op jit(solution)/shard_map/all_gather | solution.py:155
  59.9 83.0 %while.56 = (s32[]{:T(128)}, bf16[2,512,256]{2,1,0:T(8,128)(2,1)S(1)}, bf16[8,2,512,256]{3,2,1,0:T(8,128)(2,1)}, s32[]{:T(128)}, s32[]{:T(128)}, /*index=5*/s32[]{:T(128)}, s32[]{:T(128)}) while((s32[]{:T(128)}, bf16[2,512,256]{2,1,0:T(8,128)(2,1)S(1)}, bf16[8,2,512,256]{3,2,1,0:T(8,128)(2,1)}, s32[]{:T(128)}, s32[]{:T(128)}, ...), condition=%wide.region_3.4_spmd, body=%wide.region_2.3_spmd.sunk | while | flops 6 | bytes 4194471 | solution.py:107
  63.9 8.4 %collective-permute-start = (bf16[2,512,256]{2,1,0:T(8,128)(2,1)S(1)}, bf16[2,512,256]{2,1,0:T(8,128)(2,1)S(1)}, u32[]{:S(2)}, u32[]{:S(2)}) collective-permute-start(bf16[2,512,256]{2,1,0:T(8,128)(2,1)S(1)} %get-tuple-element.659), channel_id=1, source_target_pairs={{0,2},{2,4},{4,6},{6,8},{8,10},{10,12},{12,14},{14,16},{16,18},{18... | collective-permute-start | bytes 1572872 | tf_op jit(solution)/shard_map/while/body/eval_jaxpr/ppermute | solution.py:18
  74.7 9.0 %collective-permute-start = (bf16[2,512,256]{2,1,0:T(8,128)(2,1)S(1)}, bf16[2,512,256]{2,1,0:T(8,128)(2,1)S(1)}, u32[]{:S(2)}, u32[]{:S(2)}) collective-permute-start(bf16[2,512,256]{2,1,0:T(8,128)(2,1)S(1)} %get-tuple-element.659), channel_id=1, source_target_pairs={{0,2},{2,4},{4,6},{6,8},{8,10},{10,12},{12,14},{14,16},{16,18},{18... | collective-permute-start | bytes 1572872 | tf_op jit(solution)/shard_map/while/body/eval_jaxpr/ppermute | solution.py:18
  86.1 9.0 %collective-permute-start = (bf16[2,512,256]{2,1,0:T(8,128)(2,1)S(1)}, bf16[2,512,256]{2,1,0:T(8,128)(2,1)S(1)}, u32[]{:S(2)}, u32[]{:S(2)}) collective-permute-start(bf16[2,512,256]{2,1,0:T(8,128)(2,1)S(1)} %get-tuple-element.659), channel_id=1, source_target_pairs={{0,2},{2,4},{4,6},{6,8},{8,10},{10,12},{12,14},{14,16},{16,18},{18... | collective-permute-start | bytes 1572872 | tf_op jit(solution)/shard_map/while/body/eval_jaxpr/ppermute | solution.py:18
  97.4 9.0 %collective-permute-start = (bf16[2,512,256]{2,1,0:T(8,128)(2,1)S(1)}, bf16[2,512,256]{2,1,0:T(8,128)(2,1)S(1)}, u32[]{:S(2)}, u32[]{:S(2)}) collective-permute-start(bf16[2,512,256]{2,1,0:T(8,128)(2,1)S(1)} %get-tuple-element.659), channel_id=1, source_target_pairs={{0,2},{2,4},{4,6},{6,8},{8,10},{10,12},{12,14},{14,16},{16,18},{18... | collective-permute-start | bytes 1572872 | tf_op jit(solution)/shard_map/while/body/eval_jaxpr/ppermute | solution.py:18
  108.8 9.0 %collective-permute-start = (bf16[2,512,256]{2,1,0:T(8,128)(2,1)S(1)}, bf16[2,512,256]{2,1,0:T(8,128)(2,1)S(1)}, u32[]{:S(2)}, u32[]{:S(2)}) collective-permute-start(bf16[2,512,256]{2,1,0:T(8,128)(2,1)S(1)} %get-tuple-element.659), channel_id=1, source_target_pairs={{0,2},{2,4},{4,6},{6,8},{8,10},{10,12},{12,14},{14,16},{16,18},{18... | collective-permute-start | bytes 1572872 | tf_op jit(solution)/shard_map/while/body/eval_jaxpr/ppermute | solution.py:18
  120.2 9.0 %collective-permute-start = (bf16[2,512,256]{2,1,0:T(8,128)(2,1)S(1)}, bf16[2,512,256]{2,1,0:T(8,128)(2,1)S(1)}, u32[]{:S(2)}, u32[]{:S(2)}) collective-permute-start(bf16[2,512,256]{2,1,0:T(8,128)(2,1)S(1)} %get-tuple-element.659), channel_id=1, source_target_pairs={{0,2},{2,4},{4,6},{6,8},{8,10},{10,12},{12,14},{14,16},{16,18},{18... | collective-permute-start | bytes 1572872 | tf_op jit(solution)/shard_map/while/body/eval_jaxpr/ppermute | solution.py:18
  131.6 9.0 %collective-permute-start = (bf16[2,512,256]{2,1,0:T(8,128)(2,1)S(1)}, bf16[2,512,256]{2,1,0:T(8,128)(2,1)S(1)}, u32[]{:S(2)}, u32[]{:S(2)}) collective-permute-start(bf16[2,512,256]{2,1,0:T(8,128)(2,1)S(1)} %get-tuple-element.659), channel_id=1, source_target_pairs={{0,2},{2,4},{4,6},{6,8},{8,10},{10,12},{12,14},{14,16},{16,18},{18... | collective-permute-start | bytes 1572872 | tf_op jit(solution)/shard_map/while/body/eval_jaxpr/ppermute | solution.py:18
  166.5 109.6 %while.58 = (s32[]{:T(128)}, bf16[8,512,128]{1,2,0:T(8,128)(2,1)}, s32[8]{0:T(128)S(1)}, bf16[8,512,128]{1,2,0:T(8,128)(2,1)S(1)}, bf16[2,4608,128]{2,1,0:T(8,12...) while((s32[]{:T(128)}, bf16[8,512,128]{1,2,0:T(8,128)(2,1)}, ...), condition=%wide.region_8.9_spmd.clone, body=%wide.region_5.8_spmd.clone.sunk | while | flops 1238694912 | bytes 40933264 | solution.py:92
  282.4 46.2 %reduce-scatter.3.cloned.1.call-done = bf16[512,1024]{1,0:T(8,128)(2,1)} async-done(((bf16[512,2048]{1,0:T(8,128)(2,1)}), bf16[512,1024]{1,0:T(8,128)(2,1)}) %reduce-scatter.3.cloned.1.call-update) | async-done | bytes 1048592 | tf_op jit(solution)/shard_map/reduce_scatter | solution.py:169
  337.6 6.6 %copy.37 = bf16[1024,2048]{1,0:T(8,128)(2,1)} copy(bf16[1024,2048]{0,1:T(8,128)(2,1)} %get-tuple-element.470) | data formatting | bytes 8388608 | tf_op jit(solution)/shard_map/dot_general | solution.py:144
  344.2 25.8 %all-gather.5.cloned.1.call-done = bf16[512,2048]{1,0:T(8,128)(2,1)} async-done(((bf16[512,1024]{1,0:T(8,128)(2,1)}), bf16[512,2048]{1,0:T(8,128)(2,1)}) %all-gather.5.cloned.1.call-update) | async-done | bytes 2097168 | tf_op jit(solution)/shard_map/all_gather | solution.py:155
  377.6 83.0 %while.57 = (s32[]{:T(128)}, bf16[2,512,256]{2,1,0:T(8,128)(2,1)S(1)}, bf16[8,2,512,256]{3,2,1,0:T(8,128)(2,1)}, s32[]{:T(128)}, s32[]{:T(128)}, /*index=5*/s32[]{:T(128)}, s32[]{:T(128)}) while((s32[]{:T(128)}, bf16[2,512,256]{2,1,0:T(8,128)(2,1)S(1)}, bf16[8,2,512,256]{3,2,1,0:T(8,128)(2,1)}, s32[]{:T(128)}, s32[]{:T(128)}, ...), condition=%wide.region_13.14_spmd, body=%wide.region_12.13_spmd.sunk | while | flops 6 | bytes 4194471 | solution.py:107
  381.6 8.4 %collective-permute-start.1 = (bf16[2,512,256]{2,1,0:T(8,128)(2,1)S(1)}, bf16[2,512,256]{2,1,0:T(8,128)(2,1)S(1)}, u32[]{:S(2)}, u32[]{:S(2)}) collective-permute-start(bf16[2,512,256]{2,1,0:T(8,128)(2,1)S(1)} %get-tuple-element.725), channel_id=1, source_target_pairs={{0,2},{2,4},{4,6},{6,8},{8,10},{10,12},{12,14},{14,16},{16,18},{18... | collective-permute-start | bytes 1572872 | tf_op jit(solution)/shard_map/while/body/eval_jaxpr/ppermute | solution.py:18
  392.4 9.0 %collective-permute-start.1 = (bf16[2,512,256]{2,1,0:T(8,128)(2,1)S(1)}, bf16[2,512,256]{2,1,0:T(8,128)(2,1)S(1)}, u32[]{:S(2)}, u32[]{:S(2)}) collective-permute-start(bf16[2,512,256]{2,1,0:T(8,128)(2,1)S(1)} %get-tuple-element.725), channel_id=1, source_target_pairs={{0,2},{2,4},{4,6},{6,8},{8,10},{10,12},{12,14},{14,16},{16,18},{18... | collective-permute-start | bytes 1572872 | tf_op jit(solution)/shard_map/while/body/eval_jaxpr/ppermute | solution.py:18
  403.7 9.0 %collective-permute-start.1 = (bf16[2,512,256]{2,1,0:T(8,128)(2,1)S(1)}, bf16[2,512,256]{2,1,0:T(8,128)(2,1)S(1)}, u32[]{:S(2)}, u32[]{:S(2)}) collective-permute-start(bf16[2,512,256]{2,1,0:T(8,128)(2,1)S(1)} %get-tuple-element.725), channel_id=1, source_target_pairs={{0,2},{2,4},{4,6},{6,8},{8,10},{10,12},{12,14},{14,16},{16,18},{18... | collective-permute-start | bytes 1572872 | tf_op jit(solution)/shard_map/while/body/eval_jaxpr/ppermute | solution.py:18
  415.1 9.0 %collective-permute-start.1 = (bf16[2,512,256]{2,1,0:T(8,128)(2,1)S(1)}, bf16[2,512,256]{2,1,0:T(8,128)(2,1)S(1)}, u32[]{:S(2)}, u32[]{:S(2)}) collective-permute-start(bf16[2,512,256]{2,1,0:T(8,128)(2,1)S(1)} %get-tuple-element.725), channel_id=1, source_target_pairs={{0,2},{2,4},{4,6},{6,8},{8,10},{10,12},{12,14},{14,16},{16,18},{18... | collective-permute-start | bytes 1572872 | tf_op jit(solution)/shard_map/while/body/eval_jaxpr/ppermute | solution.py:18
  426.5 9.0 %collective-permute-start.1 = (bf16[2,512,256]{2,1,0:T(8,128)(2,1)S(1)}, bf16[2,512,256]{2,1,0:T(8,128)(2,1)S(1)}, u32[]{:S(2)}, u32[]{:S(2)}) collective-permute-start(bf16[2,512,256]{2,1,0:T(8,128)(2,1)S(1)} %get-tuple-element.725), channel_id=1, source_target_pairs={{0,2},{2,4},{4,6},{6,8},{8,10},{10,12},{12,14},{14,16},{16,18},{18... | collective-permute-start | bytes 1572872 | tf_op jit(solution)/shard_map/while/body/eval_jaxpr/ppermute | solution.py:18
  437.9 9.0 %collective-permute-start.1 = (bf16[2,512,256]{2,1,0:T(8,128)(2,1)S(1)}, bf16[2,512,256]{2,1,0:T(8,128)(2,1)S(1)}, u32[]{:S(2)}, u32[]{:S(2)}) collective-permute-start(bf16[2,512,256]{2,1,0:T(8,128)(2,1)S(1)} %get-tuple-element.725), channel_id=1, source_target_pairs={{0,2},{2,4},{4,6},{6,8},{8,10},{10,12},{12,14},{14,16},{16,18},{18... | collective-permute-start | bytes 1572872 | tf_op jit(solution)/shard_map/while/body/eval_jaxpr/ppermute | solution.py:18
  449.3 9.0 %collective-permute-start.1 = (bf16[2,512,256]{2,1,0:T(8,128)(2,1)S(1)}, bf16[2,512,256]{2,1,0:T(8,128)(2,1)S(1)}, u32[]{:S(2)}, u32[]{:S(2)}) collective-permute-start(bf16[2,512,256]{2,1,0:T(8,128)(2,1)S(1)} %get-tuple-element.725), channel_id=1, source_target_pairs={{0,2},{2,4},{4,6},{6,8},{8,10},{10,12},{12,14},{14,16},{16,18},{18... | collective-permute-start | bytes 1572872 | tf_op jit(solution)/shard_map/while/body/eval_jaxpr/ppermute | solution.py:18
  483.7 107.6 %while.59 = (s32[]{:T(128)}, bf16[8,512,128]{1,2,0:T(8,128)(2,1)S(1)}, s32[8]{0:T(128)S(1)}, bf16[8,512,128]{1,2,0:T(8,128)(2,1)S(1)}, bf16[2,4608,128]{2,1,0:T(...) while((s32[]{:T(128)}, ...), condition=%wide.region_17.18_spmd.clone, body=%wide.region_14.17_spmd.clone.sunk | while | flops 1238694912 | bytes 40932756 | solution.py:92
  597.2 46.3 %reduce-scatter.5.cloned.1.call-done = bf16[512,1024]{1,0:T(8,128)(2,1)} async-done(((bf16[512,2048]{1,0:T(8,128)(2,1)}), bf16[512,1024]{1,0:T(8,128)(2,1)}) %reduce-scatter.5.cloned.1.call-update) | async-done | bytes 1048592 | tf_op jit(solution)/shard_map/reduce_scatter | solution.py:169
  (273 shorter events, 304.7 us)
Async XLA Ops:
  6.5 45.8 %all-gather.3.cloned.1.call-start = ((), (), s32[]{:S(2)}) async-start(), calls=%async_computation.2 | async-start | bytes 3145728 | tf_op jit(solution)/shard_map/all_gather | solution.py:155
  17.3 311.4 %reduce-scatter.3.cloned.1.call-start = ((), (), s32[]{:S(2)}) async-start(), calls=%async_computation.3 | async-start | bytes 3145728 | tf_op jit(solution)/shard_map/reduce_scatter | solution.py:169
  25.7 6.7 %copy-start.14 = (s32[16]{0:T(128)S(1)}, s32[16]{0:T(128)}, u32[]{:S(2)}) copy-start(s32[16]{0:T(128)} %param.21) | copy-start | bytes 196
  34.4 20.2 %copy-start.5 = (f32[512,64]{0,1:T(8,128)}, f32[512,64]{0,1:T(8,128)S(1)}, u32[]{:S(2)}) copy-start(f32[512,64]{0,1:T(8,128)S(1)} %get-tuple-element.492) | copy-start | bytes 393220
  59.9 3.1 collective-permute-start
  63.9 9.9 %collective-permute-start = (bf16[2,512,256]{2,1,0:T(8,128)(2,1)S(1)}, bf16[2,512,256]{2,1,0:T(8,128)(2,1)S(1)}, u32[]{:S(2)}, u32[]{:S(2)}) collective-permute-start(bf16[2,512,256]{2,1,0:T(8,128)(2,1)S(1)} %get-tuple-element.659), channel_id=1, source_target_pairs={{0,2},{2,4},{4,6},{6,8},{8,10},{10,12},{12,14},{14,16},{16,18},{18... | collective-permute-start | bytes 1572872 | tf_op jit(solution)/shard_map/while/body/eval_jaxpr/ppermute | solution.py:18
  74.7 10.5 %collective-permute-start = (bf16[2,512,256]{2,1,0:T(8,128)(2,1)S(1)}, bf16[2,512,256]{2,1,0:T(8,128)(2,1)S(1)}, u32[]{:S(2)}, u32[]{:S(2)}) collective-permute-start(bf16[2,512,256]{2,1,0:T(8,128)(2,1)S(1)} %get-tuple-element.659), channel_id=1, source_target_pairs={{0,2},{2,4},{4,6},{6,8},{8,10},{10,12},{12,14},{14,16},{16,18},{18... | collective-permute-start | bytes 1572872 | tf_op jit(solution)/shard_map/while/body/eval_jaxpr/ppermute | solution.py:18
  86.1 10.5 %collective-permute-start = (bf16[2,512,256]{2,1,0:T(8,128)(2,1)S(1)}, bf16[2,512,256]{2,1,0:T(8,128)(2,1)S(1)}, u32[]{:S(2)}, u32[]{:S(2)}) collective-permute-start(bf16[2,512,256]{2,1,0:T(8,128)(2,1)S(1)} %get-tuple-element.659), channel_id=1, source_target_pairs={{0,2},{2,4},{4,6},{6,8},{8,10},{10,12},{12,14},{14,16},{16,18},{18... | collective-permute-start | bytes 1572872 | tf_op jit(solution)/shard_map/while/body/eval_jaxpr/ppermute | solution.py:18
  97.4 10.5 %collective-permute-start = (bf16[2,512,256]{2,1,0:T(8,128)(2,1)S(1)}, bf16[2,512,256]{2,1,0:T(8,128)(2,1)S(1)}, u32[]{:S(2)}, u32[]{:S(2)}) collective-permute-start(bf16[2,512,256]{2,1,0:T(8,128)(2,1)S(1)} %get-tuple-element.659), channel_id=1, source_target_pairs={{0,2},{2,4},{4,6},{6,8},{8,10},{10,12},{12,14},{14,16},{16,18},{18... | collective-permute-start | bytes 1572872 | tf_op jit(solution)/shard_map/while/body/eval_jaxpr/ppermute | solution.py:18
  108.8 10.5 %collective-permute-start = (bf16[2,512,256]{2,1,0:T(8,128)(2,1)S(1)}, bf16[2,512,256]{2,1,0:T(8,128)(2,1)S(1)}, u32[]{:S(2)}, u32[]{:S(2)}) collective-permute-start(bf16[2,512,256]{2,1,0:T(8,128)(2,1)S(1)} %get-tuple-element.659), channel_id=1, source_target_pairs={{0,2},{2,4},{4,6},{6,8},{8,10},{10,12},{12,14},{14,16},{16,18},{18... | collective-permute-start | bytes 1572872 | tf_op jit(solution)/shard_map/while/body/eval_jaxpr/ppermute | solution.py:18
  120.2 10.5 %collective-permute-start = (bf16[2,512,256]{2,1,0:T(8,128)(2,1)S(1)}, bf16[2,512,256]{2,1,0:T(8,128)(2,1)S(1)}, u32[]{:S(2)}, u32[]{:S(2)}) collective-permute-start(bf16[2,512,256]{2,1,0:T(8,128)(2,1)S(1)} %get-tuple-element.659), channel_id=1, source_target_pairs={{0,2},{2,4},{4,6},{6,8},{8,10},{10,12},{12,14},{14,16},{16,18},{18... | collective-permute-start | bytes 1572872 | tf_op jit(solution)/shard_map/while/body/eval_jaxpr/ppermute | solution.py:18
  131.6 10.5 %collective-permute-start = (bf16[2,512,256]{2,1,0:T(8,128)(2,1)S(1)}, bf16[2,512,256]{2,1,0:T(8,128)(2,1)S(1)}, u32[]{:S(2)}, u32[]{:S(2)}) collective-permute-start(bf16[2,512,256]{2,1,0:T(8,128)(2,1)S(1)} %get-tuple-element.659), channel_id=1, source_target_pairs={{0,2},{2,4},{4,6},{6,8},{8,10},{10,12},{12,14},{14,16},{16,18},{18... | collective-permute-start | bytes 1572872 | tf_op jit(solution)/shard_map/while/body/eval_jaxpr/ppermute | solution.py:18
  282.3 46.3 %copy-start = (bf16[512,1024]{1,0:T(8,128)(2,1)S(1)}, bf16[512,1024]{1,0:T(8,128)(2,1)}, u32[]{:S(2)}) copy-start(bf16[512,1024]{1,0:T(8,128)(2,1)} %param.15) | copy-start | bytes 3145732
  282.4 87.6 %all-gather.5.cloned.1.call-start = ((), (), s32[]{:S(2)}) async-start(), calls=%async_computation.4 | async-start | bytes 3145728 | tf_op jit(solution)/shard_map/all_gather | solution.py:155
  336.7 306.7 %reduce-scatter.5.cloned.1.call-start = ((), (), s32[]{:S(2)}) async-start(), calls=%async_computation.5 | async-start | bytes 3145728 | tf_op jit(solution)/shard_map/reduce_scatter | solution.py:169
  377.6 3.1 collective-permute-start.1
  381.6 9.9 %collective-permute-start.1 = (bf16[2,512,256]{2,1,0:T(8,128)(2,1)S(1)}, bf16[2,512,256]{2,1,0:T(8,128)(2,1)S(1)}, u32[]{:S(2)}, u32[]{:S(2)}) collective-permute-start(bf16[2,512,256]{2,1,0:T(8,128)(2,1)S(1)} %get-tuple-element.725), channel_id=1, source_target_pairs={{0,2},{2,4},{4,6},{6,8},{8,10},{10,12},{12,14},{14,16},{16,18},{18... | collective-permute-start | bytes 1572872 | tf_op jit(solution)/shard_map/while/body/eval_jaxpr/ppermute | solution.py:18
  392.4 10.5 %collective-permute-start.1 = (bf16[2,512,256]{2,1,0:T(8,128)(2,1)S(1)}, bf16[2,512,256]{2,1,0:T(8,128)(2,1)S(1)}, u32[]{:S(2)}, u32[]{:S(2)}) collective-permute-start(bf16[2,512,256]{2,1,0:T(8,128)(2,1)S(1)} %get-tuple-element.725), channel_id=1, source_target_pairs={{0,2},{2,4},{4,6},{6,8},{8,10},{10,12},{12,14},{14,16},{16,18},{18... | collective-permute-start | bytes 1572872 | tf_op jit(solution)/shard_map/while/body/eval_jaxpr/ppermute | solution.py:18
  403.7 10.5 %collective-permute-start.1 = (bf16[2,512,256]{2,1,0:T(8,128)(2,1)S(1)}, bf16[2,512,256]{2,1,0:T(8,128)(2,1)S(1)}, u32[]{:S(2)}, u32[]{:S(2)}) collective-permute-start(bf16[2,512,256]{2,1,0:T(8,128)(2,1)S(1)} %get-tuple-element.725), channel_id=1, source_target_pairs={{0,2},{2,4},{4,6},{6,8},{8,10},{10,12},{12,14},{14,16},{16,18},{18... | collective-permute-start | bytes 1572872 | tf_op jit(solution)/shard_map/while/body/eval_jaxpr/ppermute | solution.py:18
  415.1 10.5 %collective-permute-start.1 = (bf16[2,512,256]{2,1,0:T(8,128)(2,1)S(1)}, bf16[2,512,256]{2,1,0:T(8,128)(2,1)S(1)}, u32[]{:S(2)}, u32[]{:S(2)}) collective-permute-start(bf16[2,512,256]{2,1,0:T(8,128)(2,1)S(1)} %get-tuple-element.725), channel_id=1, source_target_pairs={{0,2},{2,4},{4,6},{6,8},{8,10},{10,12},{12,14},{14,16},{16,18},{18... | collective-permute-start | bytes 1572872 | tf_op jit(solution)/shard_map/while/body/eval_jaxpr/ppermute | solution.py:18
  426.5 10.5 %collective-permute-start.1 = (bf16[2,512,256]{2,1,0:T(8,128)(2,1)S(1)}, bf16[2,512,256]{2,1,0:T(8,128)(2,1)S(1)}, u32[]{:S(2)}, u32[]{:S(2)}) collective-permute-start(bf16[2,512,256]{2,1,0:T(8,128)(2,1)S(1)} %get-tuple-element.725), channel_id=1, source_target_pairs={{0,2},{2,4},{4,6},{6,8},{8,10},{10,12},{12,14},{14,16},{16,18},{18... | collective-permute-start | bytes 1572872 | tf_op jit(solution)/shard_map/while/body/eval_jaxpr/ppermute | solution.py:18
  437.9 10.5 %collective-permute-start.1 = (bf16[2,512,256]{2,1,0:T(8,128)(2,1)S(1)}, bf16[2,512,256]{2,1,0:T(8,128)(2,1)S(1)}, u32[]{:S(2)}, u32[]{:S(2)}) collective-permute-start(bf16[2,512,256]{2,1,0:T(8,128)(2,1)S(1)} %get-tuple-element.725), channel_id=1, source_target_pairs={{0,2},{2,4},{4,6},{6,8},{8,10},{10,12},{12,14},{14,16},{16,18},{18... | collective-permute-start | bytes 1572872 | tf_op jit(solution)/shard_map/while/body/eval_jaxpr/ppermute | solution.py:18
  449.3 10.5 %collective-permute-start.1 = (bf16[2,512,256]{2,1,0:T(8,128)(2,1)S(1)}, bf16[2,512,256]{2,1,0:T(8,128)(2,1)S(1)}, u32[]{:S(2)}, u32[]{:S(2)}) collective-permute-start(bf16[2,512,256]{2,1,0:T(8,128)(2,1)S(1)} %get-tuple-element.725), channel_id=1, source_target_pairs={{0,2},{2,4},{4,6},{6,8},{8,10},{10,12},{12,14},{14,16},{16,18},{18... | collective-permute-start | bytes 1572872 | tf_op jit(solution)/shard_map/while/body/eval_jaxpr/ppermute | solution.py:18
  597.1 46.3 %copy-start.2 = (bf16[512,1024]{1,0:T(8,128)(2,1)S(1)}, bf16[512,1024]{1,0:T(8,128)(2,1)}, u32[]{:S(2)}) copy-start(bf16[512,1024]{1,0:T(8,128)(2,1)} %reduce-scatter.3.cloned.1.call-done) | copy-start | bytes 3145732
  (25 other events, 51.4 us)
Sparse Core Ops, SparseCore 0:
  17.4 34.8 all-gather.2
  282.5 46.1 reduce-scatter.2
  336.8 33.0 all-gather.4
  597.3 46.1 reduce-scatter.4
where the time goes:
time: 664 us; the launch traced here: 653 us
  waiting for transfers between devices  160 us (24%)
  matrix products  144 us (22%)
  starting transfers between devices  128 us (19%)
  local copies, waits for them, and re-layouts  93.1 us (14%)
  loops' own time  60.3 us (9%)
  other arithmetic  43.4 us (7%)
  between operations  13.7 us (2%)
  blocking collectives  10.8 us (2%)
    ppermute x16, starting transfers between devices, passed_along(): lax.ppermute(value, axis, [(source, source + steps) for source in range(i...  128 us
    reduce_scatter x2, waiting for transfers between devices, per_device(): lax.psum_scatter(rounded.astype(jnp.bfloat16), 'head', scatter_dimension=...  92.5 us
    dot_general x16, matrix products, one_head(): lax.dot_general(query_one, key_one, (((1,), (1,)), ((), ())), preferred_e...  88.3 us
    another operation x2, loops' own time, attend_local(): blended = lax.map(one_head, jnp.arange(local_heads, dtype=jnp.int32))  60 us
    all_gather x2, waiting for transfers between devices, per_device(): lax.all_gather(normed_part, 'head', axis=1, tiled=True)  43.6 us
    dot_general x16, matrix products, one_head(): jnp.dot(weights, value_one, preferred_element_type=jnp.float32)  25.5 us
    ppermute x16, waiting for transfers between devices, passed_along(): lax.ppermute(value, axis, [(source, source + steps) for source in range(i...  23.6 us
    dot_general x6, local copies, waits for them, and re-layouts, project_piece(): jnp.dot(piece_rows, weight, preferred_element_type=jnp.float32)  22.5 us
  transfers between devices with their start and end apart: 20, of which 20 were waited for; matrix products, arithmetic and copies ran while one was open for 4% of the time, Pallas kernels for 0%

commit v1 on v0

--- a/solution.py
+++ b/solution.py
@@ -152,7 +152,7 @@
             jnp.zeros((rows_here, value_weight.shape[1]), jnp.float32),
         )
         query_raw, key_raw, value_raw = project_piece(
-            starting, lax.all_gather(normed_part, "head", axis=1, tiled=True), jnp.int32(0)
+            starting, jnp.concatenate(lax.all_gather(normed_part, "head"), axis=1), jnp.int32(0)
         )
         queries = rotate_heads(query_raw, token_positions, local_query)
         keys_own = rotate_heads(key_raw, token_positions, local_kv).reshape(

time: 664 us -> 681 us (1.026)
  local copies, waits for them, and re-layouts: 93.1 us -> 113 us
    reshape x0 -> x4, local copies, waits for them, and re-layouts: none -> 9.58 us  [per_device(): jnp.concatenate(lax.all_gather(normed_part, 'head'), axis=1)]
where the time goes in v1:
time: 681 us; the launch traced here: 670 us
  waiting for transfers between devices  158 us (23%)
  matrix products  140 us (21%)
  starting transfers between devices  128 us (19%)
  local copies, waits for them, and re-layouts  113 us (17%)
  loops' own time  62.9 us (9%)
  other arithmetic  43.3 us (6%)
  between operations  13.7 us (2%)
  blocking collectives  10.8 us (2%)
    ppermute x16, starting transfers between devices, passed_along(): lax.ppermute(value, axis, [(source, source + steps) for source in range(i...  128 us
    reduce_scatter x2, waiting for transfers between devices, per_device(): lax.psum_scatter(rounded.astype(jnp.bfloat16), 'head', scatter_dimension=...  92.5 us
    dot_general x16, matrix products, one_head(): lax.dot_general(query_one, key_one, (((1,), (1,)), ((), ())), preferred_e...  88.1 us
    another operation x2, loops' own time, attend_local(): blended = lax.map(one_head, jnp.arange(local_heads, dtype=jnp.int32))  62.5 us
    all_gather x2, waiting for transfers between devices, per_device(): lax.all_gather(normed_part, 'head')  42.1 us
    dot_general x16, matrix products, one_head(): jnp.dot(weights, value_one, preferred_element_type=jnp.float32)  25.5 us
    dot_general x6, local copies, waits for them, and re-layouts, project_piece(): jnp.dot(piece_rows, weight, preferred_element_type=jnp.float32)  24 us
    ppermute x16, waiting for transfers between devices, passed_along(): lax.ppermute(value, axis, [(source, source + steps) for source in range(i...  23.6 us
  transfers between devices with their start and end apart: 20, of which 20 were waited for; matrix products, arithmetic and copies ran while one was open for 4% of the time, Pallas kernels for 0%

profile of v1, /device:TPU:0, one launch (start us, length us, event | category | flops | bytes accessed | tf_op | source)
XLA Modules:
  0.0 670.0 jit_solution(1374829444870263825)
XLA Ops:
  26.5 6.6 copy.35
  35.2 17.1 %all-gather.5.cloned.1.call-done = bf16[1024,1024]{1,0:T(8,128)(2,1)} async-done(((bf16[512,1024]{1,0:T(8,128)(2,1)}), bf16[1024,1024]{1,0:T(8,128)(2,1)}) %all-gather.5.cloned.1.call-update) | async-done | bytes 2097168 | tf_op jit(solution)/shard_map/all_gather | solution.py:155
  67.5 83.0 %while.56 = (s32[]{:T(128)}, bf16[2,512,256]{2,1,0:T(8,128)(2,1)S(1)}, bf16[8,2,512,256]{3,2,1,0:T(8,128)(2,1)}, s32[]{:T(128)}, s32[]{:T(128)}, /*index=5*/s32[]{:T(128)}, s32[]{:T(128)}) while((s32[]{:T(128)}, bf16[2,512,256]{2,1,0:T(8,128)(2,1)S(1)}, bf16[8,2,512,256]{3,2,1,0:T(8,128)(2,1)}, s32[]{:T(128)}, s32[]{:T(128)}, ...), condition=%wide.region_3.4_spmd, body=%wide.region_2.3_spmd.sunk | while | flops 6 | bytes 4194471 | solution.py:107
  71.4 8.4 %collective-permute-start = (bf16[2,512,256]{2,1,0:T(8,128)(2,1)S(1)}, bf16[2,512,256]{2,1,0:T(8,128)(2,1)S(1)}, u32[]{:S(2)}, u32[]{:S(2)}) collective-permute-start(bf16[2,512,256]{2,1,0:T(8,128)(2,1)S(1)} %get-tuple-element.661), channel_id=1, source_target_pairs={{0,2},{2,4},{4,6},{6,8},{8,10},{10,12},{12,14},{14,16},{16,18},{18... | collective-permute-start | bytes 1572872 | tf_op jit(solution)/shard_map/while/body/eval_jaxpr/ppermute | solution.py:18
  82.2 9.0 %collective-permute-start = (bf16[2,512,256]{2,1,0:T(8,128)(2,1)S(1)}, bf16[2,512,256]{2,1,0:T(8,128)(2,1)S(1)}, u32[]{:S(2)}, u32[]{:S(2)}) collective-permute-start(bf16[2,512,256]{2,1,0:T(8,128)(2,1)S(1)} %get-tuple-element.661), channel_id=1, source_target_pairs={{0,2},{2,4},{4,6},{6,8},{8,10},{10,12},{12,14},{14,16},{16,18},{18... | collective-permute-start | bytes 1572872 | tf_op jit(solution)/shard_map/while/body/eval_jaxpr/ppermute | solution.py:18
  93.6 9.0 %collective-permute-start = (bf16[2,512,256]{2,1,0:T(8,128)(2,1)S(1)}, bf16[2,512,256]{2,1,0:T(8,128)(2,1)S(1)}, u32[]{:S(2)}, u32[]{:S(2)}) collective-permute-start(bf16[2,512,256]{2,1,0:T(8,128)(2,1)S(1)} %get-tuple-element.661), channel_id=1, source_target_pairs={{0,2},{2,4},{4,6},{6,8},{8,10},{10,12},{12,14},{14,16},{16,18},{18... | collective-permute-start | bytes 1572872 | tf_op jit(solution)/shard_map/while/body/eval_jaxpr/ppermute | solution.py:18
  105.0 9.0 %collective-permute-start = (bf16[2,512,256]{2,1,0:T(8,128)(2,1)S(1)}, bf16[2,512,256]{2,1,0:T(8,128)(2,1)S(1)}, u32[]{:S(2)}, u32[]{:S(2)}) collective-permute-start(bf16[2,512,256]{2,1,0:T(8,128)(2,1)S(1)} %get-tuple-element.661), channel_id=1, source_target_pairs={{0,2},{2,4},{4,6},{6,8},{8,10},{10,12},{12,14},{14,16},{16,18},{18... | collective-permute-start | bytes 1572872 | tf_op jit(solution)/shard_map/while/body/eval_jaxpr/ppermute | solution.py:18
  116.4 9.0 %collective-permute-start = (bf16[2,512,256]{2,1,0:T(8,128)(2,1)S(1)}, bf16[2,512,256]{2,1,0:T(8,128)(2,1)S(1)}, u32[]{:S(2)}, u32[]{:S(2)}) collective-permute-start(bf16[2,512,256]{2,1,0:T(8,128)(2,1)S(1)} %get-tuple-element.661), channel_id=1, source_target_pairs={{0,2},{2,4},{4,6},{6,8},{8,10},{10,12},{12,14},{14,16},{16,18},{18... | collective-permute-start | bytes 1572872 | tf_op jit(solution)/shard_map/while/body/eval_jaxpr/ppermute | solution.py:18
  127.7 9.0 %collective-permute-start = (bf16[2,512,256]{2,1,0:T(8,128)(2,1)S(1)}, bf16[2,512,256]{2,1,0:T(8,128)(2,1)S(1)}, u32[]{:S(2)}, u32[]{:S(2)}) collective-permute-start(bf16[2,512,256]{2,1,0:T(8,128)(2,1)S(1)} %get-tuple-element.661), channel_id=1, source_target_pairs={{0,2},{2,4},{4,6},{6,8},{8,10},{10,12},{12,14},{14,16},{16,18},{18... | collective-permute-start | bytes 1572872 | tf_op jit(solution)/shard_map/while/body/eval_jaxpr/ppermute | solution.py:18
  139.1 9.0 %collective-permute-start = (bf16[2,512,256]{2,1,0:T(8,128)(2,1)S(1)}, bf16[2,512,256]{2,1,0:T(8,128)(2,1)S(1)}, u32[]{:S(2)}, u32[]{:S(2)}) collective-permute-start(bf16[2,512,256]{2,1,0:T(8,128)(2,1)S(1)} %get-tuple-element.661), channel_id=1, source_target_pairs={{0,2},{2,4},{4,6},{6,8},{8,10},{10,12},{12,14},{14,16},{16,18},{18... | collective-permute-start | bytes 1572872 | tf_op jit(solution)/shard_map/while/body/eval_jaxpr/ppermute | solution.py:18
  174.1 112.1 %while.58 = (s32[]{:T(128)}, bf16[8,512,128]{1,2,0:T(8,128)(2,1)S(1)}, s32[8]{0:T(128)}, bf16[8,512,128]{1,2,0:T(8,128)(2,1)S(1)}, bf16[2,4608,128]{2,1,0:T(8,12...) while((s32[]{:T(128)}, ...), condition=%wide.region_8.9_spmd.clone, body=%wide.region_5.8_spmd.clone.sunk | while | flops 1238694912 | bytes 40932756 | solution.py:92
  292.2 46.2 %reduce-scatter.3.cloned.1.call-done = bf16[512,1024]{1,0:T(8,128)(2,1)} async-done(((bf16[512,2048]{1,0:T(8,128)(2,1)}), bf16[512,1024]{1,0:T(8,128)(2,1)}) %reduce-scatter.3.cloned.1.call-update) | async-done | bytes 1048592 | tf_op jit(solution)/shard_map/reduce_scatter | solution.py:169
  348.1 6.6 copy.43
  354.7 25.0 %all-gather.7.cloned.1.call-done = bf16[1024,1024]{1,0:T(8,128)(2,1)} async-done(((bf16[512,1024]{1,0:T(8,128)(2,1)}), bf16[1024,1024]{1,0:T(8,128)(2,1)}) %all-gather.7.cloned.1.call-update) | async-done | bytes 2097168 | tf_op jit(solution)/shard_map/all_gather | solution.py:155
  395.1 83.0 %while.57 = (s32[]{:T(128)}, bf16[2,512,256]{2,1,0:T(8,128)(2,1)S(1)}, bf16[8,2,512,256]{3,2,1,0:T(8,128)(2,1)}, s32[]{:T(128)}, s32[]{:T(128)}, /*index=5*/s32[]{:T(128)}, s32[]{:T(128)}) while((s32[]{:T(128)}, bf16[2,512,256]{2,1,0:T(8,128)(2,1)S(1)}, bf16[8,2,512,256]{3,2,1,0:T(8,128)(2,1)}, s32[]{:T(128)}, s32[]{:T(128)}, ...), condition=%wide.region_13.14_spmd, body=%wide.region_12.13_spmd.sunk | while | flops 6 | bytes 4194471 | solution.py:107
  399.0 8.4 %collective-permute-start.1 = (bf16[2,512,256]{2,1,0:T(8,128)(2,1)S(1)}, bf16[2,512,256]{2,1,0:T(8,128)(2,1)S(1)}, u32[]{:S(2)}, u32[]{:S(2)}) collective-permute-start(bf16[2,512,256]{2,1,0:T(8,128)(2,1)S(1)} %get-tuple-element.727), channel_id=1, source_target_pairs={{0,2},{2,4},{4,6},{6,8},{8,10},{10,12},{12,14},{14,16},{16,18},{18... | collective-permute-start | bytes 1572872 | tf_op jit(solution)/shard_map/while/body/eval_jaxpr/ppermute | solution.py:18
  409.8 9.0 %collective-permute-start.1 = (bf16[2,512,256]{2,1,0:T(8,128)(2,1)S(1)}, bf16[2,512,256]{2,1,0:T(8,128)(2,1)S(1)}, u32[]{:S(2)}, u32[]{:S(2)}) collective-permute-start(bf16[2,512,256]{2,1,0:T(8,128)(2,1)S(1)} %get-tuple-element.727), channel_id=1, source_target_pairs={{0,2},{2,4},{4,6},{6,8},{8,10},{10,12},{12,14},{14,16},{16,18},{18... | collective-permute-start | bytes 1572872 | tf_op jit(solution)/shard_map/while/body/eval_jaxpr/ppermute | solution.py:18
  421.2 9.0 %collective-permute-start.1 = (bf16[2,512,256]{2,1,0:T(8,128)(2,1)S(1)}, bf16[2,512,256]{2,1,0:T(8,128)(2,1)S(1)}, u32[]{:S(2)}, u32[]{:S(2)}) collective-permute-start(bf16[2,512,256]{2,1,0:T(8,128)(2,1)S(1)} %get-tuple-element.727), channel_id=1, source_target_pairs={{0,2},{2,4},{4,6},{6,8},{8,10},{10,12},{12,14},{14,16},{16,18},{18... | collective-permute-start | bytes 1572872 | tf_op jit(solution)/shard_map/while/body/eval_jaxpr/ppermute | solution.py:18
  432.6 9.0 %collective-permute-start.1 = (bf16[2,512,256]{2,1,0:T(8,128)(2,1)S(1)}, bf16[2,512,256]{2,1,0:T(8,128)(2,1)S(1)}, u32[]{:S(2)}, u32[]{:S(2)}) collective-permute-start(bf16[2,512,256]{2,1,0:T(8,128)(2,1)S(1)} %get-tuple-element.727), channel_id=1, source_target_pairs={{0,2},{2,4},{4,6},{6,8},{8,10},{10,12},{12,14},{14,16},{16,18},{18... | collective-permute-start | bytes 1572872 | tf_op jit(solution)/shard_map/while/body/eval_jaxpr/ppermute | solution.py:18
  444.0 9.0 %collective-permute-start.1 = (bf16[2,512,256]{2,1,0:T(8,128)(2,1)S(1)}, bf16[2,512,256]{2,1,0:T(8,128)(2,1)S(1)}, u32[]{:S(2)}, u32[]{:S(2)}) collective-permute-start(bf16[2,512,256]{2,1,0:T(8,128)(2,1)S(1)} %get-tuple-element.727), channel_id=1, source_target_pairs={{0,2},{2,4},{4,6},{6,8},{8,10},{10,12},{12,14},{14,16},{16,18},{18... | collective-permute-start | bytes 1572872 | tf_op jit(solution)/shard_map/while/body/eval_jaxpr/ppermute | solution.py:18
  455.4 9.0 %collective-permute-start.1 = (bf16[2,512,256]{2,1,0:T(8,128)(2,1)S(1)}, bf16[2,512,256]{2,1,0:T(8,128)(2,1)S(1)}, u32[]{:S(2)}, u32[]{:S(2)}) collective-permute-start(bf16[2,512,256]{2,1,0:T(8,128)(2,1)S(1)} %get-tuple-element.727), channel_id=1, source_target_pairs={{0,2},{2,4},{4,6},{6,8},{8,10},{10,12},{12,14},{14,16},{16,18},{18... | collective-permute-start | bytes 1572872 | tf_op jit(solution)/shard_map/while/body/eval_jaxpr/ppermute | solution.py:18
  466.7 9.0 %collective-permute-start.1 = (bf16[2,512,256]{2,1,0:T(8,128)(2,1)S(1)}, bf16[2,512,256]{2,1,0:T(8,128)(2,1)S(1)}, u32[]{:S(2)}, u32[]{:S(2)}) collective-permute-start(bf16[2,512,256]{2,1,0:T(8,128)(2,1)S(1)} %get-tuple-element.727), channel_id=1, source_target_pairs={{0,2},{2,4},{4,6},{6,8},{8,10},{10,12},{12,14},{14,16},{16,18},{18... | collective-permute-start | bytes 1572872 | tf_op jit(solution)/shard_map/while/body/eval_jaxpr/ppermute | solution.py:18
  500.6 107.6 %while.59 = (s32[]{:T(128)}, bf16[8,512,128]{1,2,0:T(8,128)(2,1)S(1)}, s32[8]{0:T(128)S(1)}, bf16[8,512,128]{1,2,0:T(8,128)(2,1)S(1)}, bf16[2,4608,128]{2,1,0:T(...) while((s32[]{:T(128)}, ...), condition=%wide.region_17.18_spmd.clone, body=%wide.region_14.17_spmd.clone.sunk | while | flops 1238694912 | bytes 40932756 | solution.py:92
  614.1 46.3 %reduce-scatter.5.cloned.1.call-done = bf16[512,1024]{1,0:T(8,128)(2,1)} async-done(((bf16[512,2048]{1,0:T(8,128)(2,1)}), bf16[512,1024]{1,0:T(8,128)(2,1)}) %reduce-scatter.5.cloned.1.call-update) | async-done | bytes 1048592 | tf_op jit(solution)/shard_map/reduce_scatter | solution.py:169
  (283 shorter events, 320.8 us)
Async XLA Ops:
  6.5 45.8 %all-gather.5.cloned.1.call-start = ((), (), s32[]{:S(2)}) async-start(), calls=%async_computation.4 | async-start | bytes 3145728 | tf_op jit(solution)/shard_map/all_gather | solution.py:155
  17.3 321.1 %reduce-scatter.3.cloned.1.call-start = ((), (), s32[]{:S(2)}) async-start(), calls=%async_computation.2 | async-start | bytes 3145728 | tf_op jit(solution)/shard_map/reduce_scatter | solution.py:169
  35.2 26.4 %copy-start.6 = (f32[512,64]{0,1:T(8,128)}, f32[512,64]{0,1:T(8,128)S(1)}, u32[]{:S(2)}) copy-start(f32[512,64]{0,1:T(8,128)S(1)} %get-tuple-element.494) | copy-start | bytes 393220
  67.5 3.1 collective-permute-start
  71.4 9.9 %collective-permute-start = (bf16[2,512,256]{2,1,0:T(8,128)(2,1)S(1)}, bf16[2,512,256]{2,1,0:T(8,128)(2,1)S(1)}, u32[]{:S(2)}, u32[]{:S(2)}) collective-permute-start(bf16[2,512,256]{2,1,0:T(8,128)(2,1)S(1)} %get-tuple-element.661), channel_id=1, source_target_pairs={{0,2},{2,4},{4,6},{6,8},{8,10},{10,12},{12,14},{14,16},{16,18},{18... | collective-permute-start | bytes 1572872 | tf_op jit(solution)/shard_map/while/body/eval_jaxpr/ppermute | solution.py:18
  82.2 10.5 %collective-permute-start = (bf16[2,512,256]{2,1,0:T(8,128)(2,1)S(1)}, bf16[2,512,256]{2,1,0:T(8,128)(2,1)S(1)}, u32[]{:S(2)}, u32[]{:S(2)}) collective-permute-start(bf16[2,512,256]{2,1,0:T(8,128)(2,1)S(1)} %get-tuple-element.661), channel_id=1, source_target_pairs={{0,2},{2,4},{4,6},{6,8},{8,10},{10,12},{12,14},{14,16},{16,18},{18... | collective-permute-start | bytes 1572872 | tf_op jit(solution)/shard_map/while/body/eval_jaxpr/ppermute | solution.py:18
  93.6 10.5 %collective-permute-start = (bf16[2,512,256]{2,1,0:T(8,128)(2,1)S(1)}, bf16[2,512,256]{2,1,0:T(8,128)(2,1)S(1)}, u32[]{:S(2)}, u32[]{:S(2)}) collective-permute-start(bf16[2,512,256]{2,1,0:T(8,128)(2,1)S(1)} %get-tuple-element.661), channel_id=1, source_target_pairs={{0,2},{2,4},{4,6},{6,8},{8,10},{10,12},{12,14},{14,16},{16,18},{18... | collective-permute-start | bytes 1572872 | tf_op jit(solution)/shard_map/while/body/eval_jaxpr/ppermute | solution.py:18
  105.0 10.5 %collective-permute-start = (bf16[2,512,256]{2,1,0:T(8,128)(2,1)S(1)}, bf16[2,512,256]{2,1,0:T(8,128)(2,1)S(1)}, u32[]{:S(2)}, u32[]{:S(2)}) collective-permute-start(bf16[2,512,256]{2,1,0:T(8,128)(2,1)S(1)} %get-tuple-element.661), channel_id=1, source_target_pairs={{0,2},{2,4},{4,6},{6,8},{8,10},{10,12},{12,14},{14,16},{16,18},{18... | collective-permute-start | bytes 1572872 | tf_op jit(solution)/shard_map/while/body/eval_jaxpr/ppermute | solution.py:18
  116.4 10.5 %collective-permute-start = (bf16[2,512,256]{2,1,0:T(8,128)(2,1)S(1)}, bf16[2,512,256]{2,1,0:T(8,128)(2,1)S(1)}, u32[]{:S(2)}, u32[]{:S(2)}) collective-permute-start(bf16[2,512,256]{2,1,0:T(8,128)(2,1)S(1)} %get-tuple-element.661), channel_id=1, source_target_pairs={{0,2},{2,4},{4,6},{6,8},{8,10},{10,12},{12,14},{14,16},{16,18},{18... | collective-permute-start | bytes 1572872 | tf_op jit(solution)/shard_map/while/body/eval_jaxpr/ppermute | solution.py:18
  127.7 10.5 %collective-permute-start = (bf16[2,512,256]{2,1,0:T(8,128)(2,1)S(1)}, bf16[2,512,256]{2,1,0:T(8,128)(2,1)S(1)}, u32[]{:S(2)}, u32[]{:S(2)}) collective-permute-start(bf16[2,512,256]{2,1,0:T(8,128)(2,1)S(1)} %get-tuple-element.661), channel_id=1, source_target_pairs={{0,2},{2,4},{4,6},{6,8},{8,10},{10,12},{12,14},{14,16},{16,18},{18... | collective-permute-start | bytes 1572872 | tf_op jit(solution)/shard_map/while/body/eval_jaxpr/ppermute | solution.py:18
  139.1 10.5 %collective-permute-start = (bf16[2,512,256]{2,1,0:T(8,128)(2,1)S(1)}, bf16[2,512,256]{2,1,0:T(8,128)(2,1)S(1)}, u32[]{:S(2)}, u32[]{:S(2)}) collective-permute-start(bf16[2,512,256]{2,1,0:T(8,128)(2,1)S(1)} %get-tuple-element.661), channel_id=1, source_target_pairs={{0,2},{2,4},{4,6},{6,8},{8,10},{10,12},{12,14},{14,16},{16,18},{18... | collective-permute-start | bytes 1572872 | tf_op jit(solution)/shard_map/while/body/eval_jaxpr/ppermute | solution.py:18
  292.1 46.3 %copy-start = (bf16[512,1024]{1,0:T(8,128)(2,1)S(1)}, bf16[512,1024]{1,0:T(8,128)(2,1)}, u32[]{:S(2)}) copy-start(bf16[512,1024]{1,0:T(8,128)(2,1)} %param.15) | copy-start | bytes 3145732
  292.1 87.6 %all-gather.7.cloned.1.call-start = ((), (), s32[]{:S(2)}) async-start(), calls=%async_computation.5 | async-start | bytes 3145728 | tf_op jit(solution)/shard_map/all_gather | solution.py:155
  338.4 6.7 copy-start.1
  346.5 314.0 %reduce-scatter.5.cloned.1.call-start = ((), (), s32[]{:S(2)}) async-start(), calls=%async_computation.3 | async-start | bytes 3145728 | tf_op jit(solution)/shard_map/reduce_scatter | solution.py:169
  395.1 3.1 collective-permute-start.1
  399.0 9.9 %collective-permute-start.1 = (bf16[2,512,256]{2,1,0:T(8,128)(2,1)S(1)}, bf16[2,512,256]{2,1,0:T(8,128)(2,1)S(1)}, u32[]{:S(2)}, u32[]{:S(2)}) collective-permute-start(bf16[2,512,256]{2,1,0:T(8,128)(2,1)S(1)} %get-tuple-element.727), channel_id=1, source_target_pairs={{0,2},{2,4},{4,6},{6,8},{8,10},{10,12},{12,14},{14,16},{16,18},{18... | collective-permute-start | bytes 1572872 | tf_op jit(solution)/shard_map/while/body/eval_jaxpr/ppermute | solution.py:18
  409.8 10.5 %collective-permute-start.1 = (bf16[2,512,256]{2,1,0:T(8,128)(2,1)S(1)}, bf16[2,512,256]{2,1,0:T(8,128)(2,1)S(1)}, u32[]{:S(2)}, u32[]{:S(2)}) collective-permute-start(bf16[2,512,256]{2,1,0:T(8,128)(2,1)S(1)} %get-tuple-element.727), channel_id=1, source_target_pairs={{0,2},{2,4},{4,6},{6,8},{8,10},{10,12},{12,14},{14,16},{16,18},{18... | collective-permute-start | bytes 1572872 | tf_op jit(solution)/shard_map/while/body/eval_jaxpr/ppermute | solution.py:18
  421.2 10.5 %collective-permute-start.1 = (bf16[2,512,256]{2,1,0:T(8,128)(2,1)S(1)}, bf16[2,512,256]{2,1,0:T(8,128)(2,1)S(1)}, u32[]{:S(2)}, u32[]{:S(2)}) collective-permute-start(bf16[2,512,256]{2,1,0:T(8,128)(2,1)S(1)} %get-tuple-element.727), channel_id=1, source_target_pairs={{0,2},{2,4},{4,6},{6,8},{8,10},{10,12},{12,14},{14,16},{16,18},{18... | collective-permute-start | bytes 1572872 | tf_op jit(solution)/shard_map/while/body/eval_jaxpr/ppermute | solution.py:18
  432.6 10.5 %collective-permute-start.1 = (bf16[2,512,256]{2,1,0:T(8,128)(2,1)S(1)}, bf16[2,512,256]{2,1,0:T(8,128)(2,1)S(1)}, u32[]{:S(2)}, u32[]{:S(2)}) collective-permute-start(bf16[2,512,256]{2,1,0:T(8,128)(2,1)S(1)} %get-tuple-element.727), channel_id=1, source_target_pairs={{0,2},{2,4},{4,6},{6,8},{8,10},{10,12},{12,14},{14,16},{16,18},{18... | collective-permute-start | bytes 1572872 | tf_op jit(solution)/shard_map/while/body/eval_jaxpr/ppermute | solution.py:18
  444.0 10.5 %collective-permute-start.1 = (bf16[2,512,256]{2,1,0:T(8,128)(2,1)S(1)}, bf16[2,512,256]{2,1,0:T(8,128)(2,1)S(1)}, u32[]{:S(2)}, u32[]{:S(2)}) collective-permute-start(bf16[2,512,256]{2,1,0:T(8,128)(2,1)S(1)} %get-tuple-element.727), channel_id=1, source_target_pairs={{0,2},{2,4},{4,6},{6,8},{8,10},{10,12},{12,14},{14,16},{16,18},{18... | collective-permute-start | bytes 1572872 | tf_op jit(solution)/shard_map/while/body/eval_jaxpr/ppermute | solution.py:18
  455.4 10.5 %collective-permute-start.1 = (bf16[2,512,256]{2,1,0:T(8,128)(2,1)S(1)}, bf16[2,512,256]{2,1,0:T(8,128)(2,1)S(1)}, u32[]{:S(2)}, u32[]{:S(2)}) collective-permute-start(bf16[2,512,256]{2,1,0:T(8,128)(2,1)S(1)} %get-tuple-element.727), channel_id=1, source_target_pairs={{0,2},{2,4},{4,6},{6,8},{8,10},{10,12},{12,14},{14,16},{16,18},{18... | collective-permute-start | bytes 1572872 | tf_op jit(solution)/shard_map/while/body/eval_jaxpr/ppermute | solution.py:18
  466.7 10.5 %collective-permute-start.1 = (bf16[2,512,256]{2,1,0:T(8,128)(2,1)S(1)}, bf16[2,512,256]{2,1,0:T(8,128)(2,1)S(1)}, u32[]{:S(2)}, u32[]{:S(2)}) collective-permute-start(bf16[2,512,256]{2,1,0:T(8,128)(2,1)S(1)} %get-tuple-element.727), channel_id=1, source_target_pairs={{0,2},{2,4},{4,6},{6,8},{8,10},{10,12},{12,14},{14,16},{16,18},{18... | collective-permute-start | bytes 1572872 | tf_op jit(solution)/shard_map/while/body/eval_jaxpr/ppermute | solution.py:18
  614.1 46.3 %copy-start.2 = (bf16[512,1024]{1,0:T(8,128)(2,1)S(1)}, bf16[512,1024]{1,0:T(8,128)(2,1)}, u32[]{:S(2)}) copy-start(bf16[512,1024]{1,0:T(8,128)(2,1)} %reduce-scatter.3.cloned.1.call-done) | copy-start | bytes 3145732
  (27 other events, 57.1 us)
Sparse Core Ops, SparseCore 0:
  17.4 34.8 all-gather.4
  292.2 46.1 reduce-scatter.2
  346.6 33.0 all-gather.6
  614.3 46.1 reduce-scatter.4
